TPU v7x, 512 devices: a whole 4x8x8 slice. The times are simulated.
512 devices in a mesh: head: 4 (over x), blk: 128 (over y, z, core).
Axes of the slice: x: 4, y: 8, z: 8, core: 2. Of those that a mesh axis runs over, the one named last changes fastest.
Arguments:
- tokens: bfloat16 [8192, 2048], P('blk'), may hold values from -6 to 6
- q_weight: bfloat16 [2048, 1024], P(None, 'head')
- k_weight: bfloat16 [2048, 256], P(None, 'head')
- v_weight: bfloat16 [2048, 256], P(None, 'head'), may hold values from -0.125 to 0.125
- o_weight: bfloat16 [1024, 2048], P('head'), may hold values from -0.1875 to 0.1875
- kv_pages: bfloat16 [4, 384, 64, 128], P('head', 'blk')
- page_node: int32 [384], replicated, may hold values from 0 to 72, as said below
- page_fill: int32 [384], replicated, may hold values from 1 to 64
- req_len: int32 [64], replicated, may hold values from 1 to 256, 8192 in all
- req_leaf: int32 [64], replicated, may hold values from 0 to 63
- leaf_parent: int32 [64], replicated, may hold values from 0 to 7
Outputs:
- attn_out: bfloat16 [8192, 2048], P('blk', 'head')
Inputs may be any that keep to these rules, and one draw needn't show every extreme that they name: `req_len`: their sum is 8192, and the longest request has exactly 256 tokens. `page_node`: node 0 is the root, nodes 1 to 8 form the middle level and the rest are leaves; the root holds a third of the 384 pages, each middle node a 1 / 8 share of another third, each leaf two pages, placed over the pages in any order.
All inputs are finite; a program needn't handle non-finite values.
Results may differ from a plain program's by a relative error of at most 0.012.
The roundings to bfloat16 on the way count: a program that leaves them out, or rounds other values in their place, can miss the bound.
Values may be sent and summed in bfloat16 or wider, within the bound.
A program may use at most 128 MiB of HBM per device.

v0:
```python
import jax
import jax.numpy as jnp
from jax import lax
from jax.sharding import PartitionSpec as P

HD = 64
MIDS = 8
PROMPT = 256
NEGATIVE = -1e30
EPSILON = 1e-06
ROPE_BASE = 10000.0
SCORE_SCALE = 0.125


def shifted(value, axis, steps):
    count = lax.axis_size(axis)
    first, last = (max(0, -steps), min(count, count - steps))
    return lax.ppermute(value, axis, [(source, source + steps) for source in range(first, last)])


def norm_rows(hidden):
    wide = hidden.astype(jnp.float32)
    return (wide * lax.rsqrt(jnp.mean(wide * wide, axis=-1, keepdims=True) + EPSILON)).astype(
        jnp.bfloat16
    )


def rotate(values, positions):
    half_dim = values.shape[-1] // 2
    frequency = ROPE_BASE ** (-jnp.arange(half_dim).astype(jnp.float32) / half_dim)
    angles = positions.astype(jnp.float32)[:, None] * frequency[None, :]
    cosine = jnp.cos(angles)[:, None, :]
    sine_part = jnp.sin(angles)[:, None, :]
    first_half = values[..., :half_dim]
    second = values[..., half_dim:]
    return jnp.concatenate(
        [first_half * cosine - second * sine_part, second * cosine + first_half * sine_part],
        axis=-1,
    )


def request_of(places, req_len):
    req_end = jnp.cumsum(req_len)
    return jnp.sum((places[:, None] >= req_end[None, :]).astype(jnp.int32), axis=1)


def row_paths(places, req_len, req_leaf, leaf_parent, page_node, page_fill):
    req_count = req_len.shape[0]
    leaf_count = leaf_parent.shape[0]
    node_count = 1 + MIDS + leaf_count
    starts = jnp.cumsum(req_len) - req_len
    request = request_of(places, req_len)
    chosen = request[:, None] == jnp.arange(req_count, dtype=jnp.int32)[None, :]
    offset = places - jnp.sum(jnp.where(chosen, starts[None, :], 0), axis=1)
    leaf_id = jnp.sum(jnp.where(chosen, req_leaf[None, :], 0), axis=1)
    leaf_hit = leaf_id[:, None] == jnp.arange(leaf_count, dtype=jnp.int32)[None, :]
    mid_id = jnp.sum(jnp.where(leaf_hit, leaf_parent[None, :], 0), axis=1)
    path_ids = jnp.stack([jnp.zeros_like(mid_id), 1 + mid_id, 1 + MIDS + leaf_id], axis=1)
    node_hit = page_node[:, None] == jnp.arange(node_count, dtype=jnp.int32)[None, :]
    node_len = jnp.sum(jnp.where(node_hit, page_fill[:, None], 0), axis=0)
    on_path = path_ids[:, :, None] == jnp.arange(node_count, dtype=jnp.int32)[None, None, :]
    prefix = jnp.sum(jnp.where(on_path, node_len[None, None, :], 0), axis=(1, 2))
    return (request, path_ids, prefix + offset)


def page_mask(path_ids, nodes_here, fills_here, page_len):
    node_hit = jnp.any(path_ids[:, :, None] == nodes_here[None, None, :], axis=1)
    slot_live = jnp.arange(page_len, dtype=jnp.int32)[None, :] < fills_here[:, None]
    return (node_hit[:, :, None] & slot_live[None, :, :]).reshape(path_ids.shape[0], -1)


def block_size(total_pages, page_limit):
    chosen = 1
    for trial_size in range(1, min(total_pages, page_limit) + 1):
        if total_pages % trial_size == 0:
            chosen = trial_size
    return chosen


def fold_keys(running, q_rot, key_rows, values, allowed):
    top_old, total_old, accum_old = running
    scores = (
        jnp.einsum("rkhd,knd->khrn", q_rot, key_rows, preferred_element_type=jnp.float32)
        * SCORE_SCALE
    )
    scores = jnp.where(allowed[None, None], scores, NEGATIVE)
    top_new = jnp.maximum(top_old, jnp.max(scores, axis=-1))
    weights = jnp.where(allowed[None, None], jnp.exp(scores - top_new[..., None]), 0.0)
    factor = jnp.exp(top_old - top_new)
    total_new = total_old * factor + jnp.sum(weights, axis=-1)
    product = jnp.einsum(
        "khrn,knd->khrd", weights.astype(jnp.bfloat16), values, preferred_element_type=jnp.float32
    )
    return (top_new, total_new, accum_old * factor[..., None] + product)


def local(
    tokens,
    q_weight,
    k_weight,
    v_weight,
    o_weight,
    kv_pages,
    page_node,
    page_fill,
    req_len,
    req_leaf,
    leaf_parent,
):
    local_rows = tokens.shape[0]
    kv_heads = k_weight.shape[1] // HD
    q_heads = q_weight.shape[1] // HD
    group_size = q_heads // kv_heads
    page_len = kv_pages.shape[2]
    blk_index = lax.axis_index("blk")
    places = blk_index * local_rows + jnp.arange(local_rows, dtype=jnp.int32)
    request, path_ids, positions = row_paths(
        places, req_len, req_leaf, leaf_parent, page_node, page_fill
    )
    normed = norm_rows(tokens)
    queries = jnp.dot(normed, q_weight, preferred_element_type=jnp.float32).reshape(
        local_rows, q_heads, HD
    )
    q_rot = (
        rotate(queries, positions)
        .astype(jnp.bfloat16)
        .reshape(local_rows, kv_heads, group_size, HD)
    )
    keys_new = jnp.dot(normed, k_weight, preferred_element_type=jnp.float32).reshape(
        local_rows, kv_heads, HD
    )
    keys_new = rotate(keys_new, positions).astype(jnp.bfloat16)
    values_new = (
        jnp.dot(normed, v_weight, preferred_element_type=jnp.float32)
        .astype(jnp.bfloat16)
        .reshape(local_rows, kv_heads, HD)
    )
    own_pack = jnp.concatenate([keys_new, values_new], axis=-1)
    reach_devs = (PROMPT - 1) // local_rows + 1
    near_packs = [own_pack]
    near_places = [places]
    for distance in range(1, reach_devs + 1):
        near_packs.insert(0, shifted(own_pack, "blk", distance))
        near_places.insert(0, places - distance * local_rows)
    near_pack = jnp.swapaxes(jnp.concatenate(near_packs, axis=0), 0, 1)
    near_place = jnp.concatenate(near_places)
    near_req = request_of(jnp.maximum(near_place, 0), req_len)
    near_ok = (
        (near_place[None, :] >= 0)
        & (near_req[None, :] == request[:, None])
        & (near_place[None, :] <= places[:, None])
    )
    start_state = (
        jnp.full((kv_heads, group_size, local_rows), NEGATIVE, jnp.float32),
        jnp.zeros((kv_heads, group_size, local_rows), jnp.float32),
        jnp.zeros((kv_heads, group_size, local_rows, HD), jnp.float32),
    )
    running = fold_keys(start_state, q_rot, near_pack[..., :HD], near_pack[..., HD:], near_ok)
    group_limit = max(1, 2048 // page_len)
    shard_pages = lax.all_gather(kv_pages, "blk", axis=1, tiled=True)
    page_total = shard_pages.shape[1]
    group_pages = block_size(page_total, group_limit)

    def one_group(group_index, inner):
        first_page = group_index * group_pages
        page_block = lax.dynamic_slice_in_dim(shard_pages, first_page, group_pages, 1)
        nodes_here = lax.dynamic_slice_in_dim(page_node, first_page, group_pages, 0)
        fills_here = lax.dynamic_slice_in_dim(page_fill, first_page, group_pages, 0)
        allowed = page_mask(path_ids, nodes_here, fills_here, page_len)
        flat_block = page_block.reshape(kv_heads, group_pages * page_len, 2 * HD)
        return fold_keys(inner, q_rot, flat_block[..., :HD], flat_block[..., HD:], allowed)

    running = lax.fori_loop(0, page_total // group_pages, one_group, running)
    top_all, total_all, accum_all = running
    attended = accum_all / total_all[..., None]
    attended = (
        jnp.transpose(attended, (2, 0, 1, 3)).reshape(local_rows, q_heads * HD).astype(jnp.bfloat16)
    )
    partial_out = jnp.dot(attended, o_weight, preferred_element_type=jnp.float32)
    return lax.psum_scatter(partial_out, "head", scatter_dimension=1, tiled=True).astype(
        jnp.bfloat16
    )


def solution(mesh):
    return jax.shard_map(
        local,
        mesh=mesh,
        in_specs=(
            P("blk", None),
            P(None, "head"),
            P(None, "head"),
            P(None, "head"),
            P("head", None),
            P("head", "blk", None, None),
            P(),
            P(),
            P(),
            P(),
            P(),
        ),
        out_specs=P("blk", "head"),
        check_vma=False,
    )
```

profile of v0, /device:TPU:8, one launch (start us, length us, event | category | flops | bytes accessed | tf_op | source)
XLA Modules:
  0.0 205.3 jit_solution(11109464322911127699)
XLA Ops:
  9.1 0.8 select_reduce_fusion.2
  10.0 0.8 select_reduce_fusion.3
  10.8 0.8 select_reduce_fusion
  11.9 1.1 fusion.17
  13.1 1.3 convolution_bitcast_fusion.1
  14.8 1.3 fusion.16
  16.2 1.9 collective-permute-start.3
  18.1 4.3 %collective-permute-start.2 = (bf16[64,1,128]{2,0,1:T(8,128)(2,1)S(1)}, bf16[64,1,128]{2,0,1:T(8,128)(2,1)S(1)}, u32[]{:S(2)}, u32[]{:S(2)}) collective-permute-start(bf16[64,1,128]{2,0,1:T(8,128)(2,1)S(1)} %pad_maximum_fusion.1), channel_id=1, source_target_pairs={{0,2},{1,3},{2,4},{3,5},{4,6},{5,7},{6,8},{7,9},{8,10},{9,11},{10,... | collective-permute-start | bytes 49160 | tf_op jit(solution)/shard_map/ppermute | solution.py:18
  22.4 6.1 %collective-permute-start.1 = (bf16[64,1,128]{2,0,1:T(8,128)(2,1)S(1)}, bf16[64,1,128]{2,0,1:T(8,128)(2,1)S(1)}, u32[]{:S(2)}, u32[]{:S(2)}) collective-permute-start(bf16[64,1,128]{2,0,1:T(8,128)(2,1)S(1)} %pad_maximum_fusion.1), channel_id=1, source_target_pairs={{0,3},{1,4},{2,5},{3,6},{4,7},{5,8},{6,9},{7,10},{8,11},{9,12},{10... | collective-permute-start | bytes 49160 | tf_op jit(solution)/shard_map/ppermute | solution.py:18
  28.5 6.4 %collective-permute-start = (bf16[64,1,128]{2,0,1:T(8,128)(2,1)S(1)}, bf16[64,1,128]{2,0,1:T(8,128)(2,1)S(1)}, u32[]{:S(2)}, u32[]{:S(2)}) collective-permute-start(bf16[64,1,128]{2,0,1:T(8,128)(2,1)S(1)} %pad_maximum_fusion.1), channel_id=1, source_target_pairs={{0,4},{1,5},{2,6},{3,7},{4,8},{5,9},{6,10},{7,11},{8,12},{9,13},{1... | collective-permute-start | bytes 49160 | tf_op jit(solution)/shard_map/ppermute | solution.py:18
  34.9 1.7 fusion.41
  38.5 62.9 %all-gather.2.cloned.1.call-done = bf16[1,384,64,128]{3,2,0,1:T(8,128)(2,1)} async-done(((bf16[1,3,64,128]{3,2,0,1:T(8,128)(2,1)}), bf16[1,384,64,128]{3,2,0,1:T(8,128)(2,1)}) %all-gather.2.cloned.1.call-update) | async-done | bytes 6291472 | tf_op jit(solution)/shard_map/all_gather | solution.py:160
  101.3 70.1 %while.17 = (s32[]{:T(128)}, f32[1,4,64]{2,1,0:T(4,128)S(1)}, f32[1,4,64]{2,1,0:T(4,128)S(1)}, f32[1,4,64,64]{3,2,1,0:T(8,128)S(1)}, s32[64,3]{0,1:T(4,128)S(1)}...) while((s32[]{:T(128)}, f32[1,4,64]{2,1,0:T(4,128)S(1)}, ...), condition=%wide.region_15.16_spmd, body=%wide.region_11.15_spmd.sunk | while | flops 139113216 | bytes 9696951 | solution.py:173
  104.2 1.1 constant_dynamic-slice_fusion.2
  107.2 0.8 dynamic_slice.27
  110.1 1.1 constant_dynamic-slice_fusion.2
  113.0 0.8 dynamic_slice.27
  115.9 1.1 constant_dynamic-slice_fusion.2
  121.8 1.1 constant_dynamic-slice_fusion.2
  124.7 0.8 dynamic_slice.27
  127.6 1.1 constant_dynamic-slice_fusion.2
  133.4 1.1 constant_dynamic-slice_fusion.2
  139.3 1.1 constant_dynamic-slice_fusion.2
  145.1 1.1 constant_dynamic-slice_fusion.2
  151.0 1.1 constant_dynamic-slice_fusion.2
  156.8 1.1 constant_dynamic-slice_fusion.2
  162.7 1.1 constant_dynamic-slice_fusion.2
  165.6 0.8 dynamic_slice.27
  168.5 1.1 constant_dynamic-slice_fusion.2
  171.7 1.1 fusion.48
  172.8 24.0 %reduce-scatter.2.cloned.1.call-done = f32[64,512]{1,0:T(8,128)} async-done(((f32[64,2048]{1,0:T(8,128)}), f32[64,512]{1,0:T(8,128)}) %reduce-scatter.2.cloned.1.call-update) | async-done | bytes 131088 | tf_op jit(solution)/shard_map/reduce_scatter | solution.py:180
  196.9 1.5 convert_element_type.84
  (265 shorter events, 58.6 us)
Async XLA Ops:
  6.5 165.2 %copy-start = (bf16[256,2048]{1,0:T(8,128)(2,1)S(1)}, bf16[256,2048]{1,0:T(8,128)(2,1)}, u32[]{:S(2)}) copy-start(bf16[256,2048]{1,0:T(8,128)(2,1)} %param.17) | copy-start | bytes 3145732
  6.5 94.8 %all-gather.2.cloned.1.call-start = ((), (), s32[]{:S(2)}) async-start(), calls=%async_computation.1 | async-start | bytes 6340608 | tf_op jit(solution)/shard_map/all_gather | solution.py:160
  7.3 189.6 %reduce-scatter.2.cloned.1.call-start = ((), (), s32[]{:S(2)}) async-start(), calls=%async_computation.2 | async-start | bytes 655360 | tf_op jit(solution)/shard_map/reduce_scatter | solution.py:180
  16.2 21.4 %collective-permute-start.3 = (bf16[64,1,128]{2,0,1:T(8,128)(2,1)S(1)}, bf16[64,1,128]{2,0,1:T(8,128)(2,1)S(1)}, u32[]{:S(2)}, u32[]{:S(2)}) collective-permute-start(bf16[64,1,128]{2,0,1:T(8,128)(2,1)S(1)} %pad_maximum_fusion.1), channel_id=1, source_target_pairs={{0,1},{1,2},{2,3},{3,4},{4,5},{5,6},{6,7},{7,8},{8,9},{9,10},{10,1... | collective-permute-start | bytes 49160 | tf_op jit(solution)/shard_map/ppermute | solution.py:18
  18.1 19.4 %collective-permute-start.2 = (bf16[64,1,128]{2,0,1:T(8,128)(2,1)S(1)}, bf16[64,1,128]{2,0,1:T(8,128)(2,1)S(1)}, u32[]{:S(2)}, u32[]{:S(2)}) collective-permute-start(bf16[64,1,128]{2,0,1:T(8,128)(2,1)S(1)} %pad_maximum_fusion.1), channel_id=1, source_target_pairs={{0,2},{1,3},{2,4},{3,5},{4,6},{5,7},{6,8},{7,9},{8,10},{9,11},{10,... | collective-permute-start | bytes 49160 | tf_op jit(solution)/shard_map/ppermute | solution.py:18
  22.4 15.1 %collective-permute-start.1 = (bf16[64,1,128]{2,0,1:T(8,128)(2,1)S(1)}, bf16[64,1,128]{2,0,1:T(8,128)(2,1)S(1)}, u32[]{:S(2)}, u32[]{:S(2)}) collective-permute-start(bf16[64,1,128]{2,0,1:T(8,128)(2,1)S(1)} %pad_maximum_fusion.1), channel_id=1, source_target_pairs={{0,3},{1,4},{2,5},{3,6},{4,7},{5,8},{6,9},{7,10},{8,11},{9,12},{10... | collective-permute-start | bytes 49160 | tf_op jit(solution)/shard_map/ppermute | solution.py:18
  28.5 9.0 %collective-permute-start = (bf16[64,1,128]{2,0,1:T(8,128)(2,1)S(1)}, bf16[64,1,128]{2,0,1:T(8,128)(2,1)S(1)}, u32[]{:S(2)}, u32[]{:S(2)}) collective-permute-start(bf16[64,1,128]{2,0,1:T(8,128)(2,1)S(1)} %pad_maximum_fusion.1), channel_id=1, source_target_pairs={{0,4},{1,5},{2,6},{3,7},{4,8},{5,9},{6,10},{7,11},{8,12},{9,13},{1... | collective-permute-start | bytes 49160 | tf_op jit(solution)/shard_map/ppermute | solution.py:18
Sparse Core Ops, SparseCore 0:
  10.5 90.7 all-gather.1
  173.0 23.8 reduce-scatter.1
where the time goes:
time: 207 us; the launch traced here: 205 us
  waiting for transfers between devices  87.6 us (42%)
  local copies, waits for them, and re-layouts  47 us (23%)
  matrix products  21.1 us (10%)
  starting transfers between devices  18.7 us (9%)
  other arithmetic  16.3 us (8%)
  between operations  13.7 us (7%)
    all_gather x1, waiting for transfers between devices, local(): shard_pages = lax.all_gather(kv_pages, 'blk', axis=1, tiled=True)  62.9 us
    reduce_scatter x1, waiting for transfers between devices, local(): lax.psum_scatter(partial_out, 'head', scatter_dimension=1, tiled=True)  24 us
    ppermute x4, starting transfers between devices, shifted(): lax.ppermute(value, axis, [(source, source + steps) for source in range(f...  18.7 us
    dynamic_slice x12, local copies, waits for them, and re-layouts, one_group(): lax.dynamic_slice_in_dim(shard_pages, first_page, group_pages, 1)  13 us
    and x24, local copies, waits for them, and re-layouts, page_mask(): node_hit[:, :, None] & slot_live[None, :, :]  9.91 us
    dynamic_slice x12, local copies, waits for them, and re-layouts, one_group(): fills_here = lax.dynamic_slice_in_dim(page_fill, first_page, group_pages, 0)  9.1 us
    dynamic_slice x12, local copies, waits for them, and re-layouts, one_group(): nodes_here = lax.dynamic_slice_in_dim(page_node, first_page, group_pages, 0)  9.04 us
    dot_general x13, matrix products, fold_keys(): jnp.einsum('khrn,knd->khrd', weights.astype(jnp.bfloat16), values, prefer...  8.63 us
  transfers between devices with their start and end apart: 6, of which 2 were waited for; matrix products, arithmetic and copies ran while one was open for 6% of the time, Pallas kernels for 0%

commit v1 on v0

--- a/solution.py
+++ b/solution.py
@@ -10,6 +10,11 @@
 EPSILON = 1e-06
 ROPE_BASE = 10000.0
 SCORE_SCALE = 0.125
+
+
+def all_by_exchange(block, axis, dim):
+    sent = jnp.stack([block] * lax.axis_size(axis))
+    return jnp.concatenate(lax.all_to_all(sent, axis, 0, 0), axis=dim)
 
 
 def shifted(value, axis, steps):
@@ -157,7 +162,7 @@
     )
     running = fold_keys(start_state, q_rot, near_pack[..., :HD], near_pack[..., HD:], near_ok)
     group_limit = max(1, 2048 // page_len)
-    shard_pages = lax.all_gather(kv_pages, "blk", axis=1, tiled=True)
+    shard_pages = all_by_exchange(kv_pages, "blk", 1)
     page_total = shard_pages.shape[1]
     group_pages = block_size(page_total, group_limit)
 

time: 207 us -> 303 us (1.46)
  waiting for transfers between devices: 87.6 us -> 189 us
  starting transfers between devices: 18.7 us -> 32 us
  local copies, waits for them, and re-layouts: 47 us -> 35.2 us
  other arithmetic: 16.3 us -> 12.7 us
  matrix products: 21.1 us -> 17.8 us
    ppermute x4, waiting for transfers between devices: 0.01 us -> 137 us  [shifted(): lax.ppermute(value, axis, [(source, source + steps) for source in range(f...]
    all_gather x1 -> x0, waiting for transfers between devices: 62.9 us -> none  [local(): shard_pages = lax.all_gather(kv_pages, 'blk', axis=1, tiled=True)]
    reduce_scatter x1, waiting for transfers between devices: 24 us -> 51.7 us  [local(): lax.psum_scatter(partial_out, 'head', scatter_dimension=1, tiled=True)]
    all_to_all x0 -> x1, starting transfers between devices: none -> 17.9 us  [all_by_exchange(): return jnp.concatenate(lax.all_to_all(sent, axis, 0, 0), axis=dim)]
    dynamic_slice x12, local copies, waits for them, and re-layouts: 9.1 us -> 0.95 us  [one_group(): fills_here = lax.dynamic_slice_in_dim(page_fill, first_page, group_pages, 0)]
    dynamic_slice x12, local copies, waits for them, and re-layouts: 9.04 us -> 0.92 us  [one_group(): nodes_here = lax.dynamic_slice_in_dim(page_node, first_page, group_pages, 0)]
    ppermute x4, starting transfers between devices: 18.7 us -> 14 us  [shifted(): lax.ppermute(value, axis, [(source, source + steps) for source in range(f...]
    another operation x3 -> x4, local copies, waits for them, and re-layouts: 0.94 us -> 5.44 us  [the longest x1 5.15 us: all_by_exchange(): sent = jnp.stack([block] * lax.axis_size(axis))]
  transfers between devices with their start and end apart: 6 -> 6, of which waited for: 2 -> 3; matrix products, arithmetic and copies ran while one was open for 6% -> 1% of each run, Pallas kernels for 0% -> 0%
where the time goes in v1:
time: 303 us; the launch traced here: 302 us
  waiting for transfers between devices  189 us (62%)
  local copies, waits for them, and re-layouts  35.2 us (12%)
  starting transfers between devices  32 us (11%)
  matrix products  17.8 us (6%)
  between operations  13.8 us (5%)
  other arithmetic  12.7 us (4%)
    ppermute x4, waiting for transfers between devices, shifted(): lax.ppermute(value, axis, [(source, source + steps) for source in range(f...  137 us
    reduce_scatter x1, waiting for transfers between devices, local(): lax.psum_scatter(partial_out, 'head', scatter_dimension=1, tiled=True)  51.7 us
    all_to_all x1, starting transfers between devices, all_by_exchange(): return jnp.concatenate(lax.all_to_all(sent, axis, 0, 0), axis=dim)  17.9 us
    ppermute x4, starting transfers between devices, shifted(): lax.ppermute(value, axis, [(source, source + steps) for source in range(f...  14 us
    dynamic_slice x12, local copies, waits for them, and re-layouts, one_group(): lax.dynamic_slice_in_dim(shard_pages, first_page, group_pages, 1)  13 us
    and x24, local copies, waits for them, and re-layouts, page_mask(): node_hit[:, :, None] & slot_live[None, :, :]  9.92 us
    dot_general x13, matrix products, fold_keys(): jnp.einsum('khrn,knd->khrd', weights.astype(jnp.bfloat16), values, prefer...  8.64 us
    dot_general x13, matrix products, fold_keys(): jnp.einsum('rkhd,knd->khrn', q_rot, key_rows, preferred_element_type=jnp....  7.2 us
  transfers between devices with their start and end apart: 6, of which 3 were waited for; matrix products, arithmetic and copies ran while one was open for 1% of the time, Pallas kernels for 0%

profile of v1, /device:TPU:8, one launch (start us, length us, event | category | flops | bytes accessed | tf_op | source)
XLA Modules:
  0.0 301.7 jit_solution(8424905000816628908)
XLA Ops:
  6.5 5.1 %stack.5 = bf16[128,1,3,64,128]{4,3,2,1,0:T(8,128)(2,1)} broadcast(bf16[3,64,128]{2,1,0:T(8,128)(2,1)} %bitcast.119), dimensions={2,3,4} | broadcast | bytes 6340608 | tf_op jit(solution)/shard_map/stack | solution.py:16
  11.8 17.9 %all-to-all-start = ((bf16[128,1,3,64,128]{4,3,2,1,0:T(8,128)(2,1)}), bf16[128,1,3,64,128]{4,3,2,1,0:T(8,128)(2,1)}, u32[]{:S(2)}, u32[]{:S(2)}) async-start(bf16[128,1,3,64,128]{4,3,2,1,0:T(8,128)(2,1)} %stack.5), calls=%async_computation | async-start | bytes 12582912 | tf_op jit(solution)/shard_map/all_to_all | solution.py:17
  32.3 4.3 %collective-permute-start = (bf16[64,1,128]{2,0,1:T(8,128)(2,1)S(1)}, bf16[64,1,128]{2,0,1:T(8,128)(2,1)S(1)}, u32[]{:S(2)}, u32[]{:S(2)}) collective-permute-start(bf16[64,1,128]{2,0,1:T(8,128)(2,1)S(1)} %pad_maximum_fusion.1), channel_id=1, source_target_pairs={{0,4},{1,5},{2,6},{3,7},{4,8},{5,9},{6,10},{7,11},{8,12},{9,13},{1... | collective-permute-start | bytes 49160 | tf_op jit(solution)/shard_map/ppermute | solution.py:23
  36.6 2.9 collective-permute-start.1
  39.5 4.6 %collective-permute-start.2 = (bf16[64,1,128]{2,0,1:T(8,128)(2,1)S(1)}, bf16[64,1,128]{2,0,1:T(8,128)(2,1)S(1)}, u32[]{:S(2)}, u32[]{:S(2)}) collective-permute-start(bf16[64,1,128]{2,0,1:T(8,128)(2,1)S(1)} %pad_maximum_fusion.1), channel_id=1, source_target_pairs={{0,2},{1,3},{2,4},{3,5},{4,6},{5,7},{6,8},{7,9},{8,10},{9,11},{10,... | collective-permute-start | bytes 49160 | tf_op jit(solution)/shard_map/ppermute | solution.py:23
  44.1 2.3 collective-permute-start.3
  47.6 136.8 %collective-permute-done = bf16[64,1,128]{2,0,1:T(8,128)(2,1)S(1)} collective-permute-done((bf16[64,1,128]{2,0,1:T(8,128)(2,1)S(1)}, bf16[64,1,128]{2,0,1:T(8,128)(2,1)S(1)}, u32[]{:S(2)}, u32[]{:S(2)}) %collective-permute-start) | collective-permute-done | bytes 16416 | tf_op jit(solution)/shard_map/ppermute | solution.py:23
  185.4 0.8 all-to-all-done
  186.2 54.0 %while.17 = (s32[]{:T(128)}, f32[1,4,64]{2,1,0:T(4,128)S(1)}, f32[1,4,64]{2,1,0:T(4,128)S(1)}, f32[1,4,64,64]{3,2,1,0:T(8,128)S(1)}, s32[64,3]{0,1:T(4,128)S(1)}...) while((s32[]{:T(128)}, f32[1,4,64]{2,1,0:T(4,128)S(1)}, ...), condition=%wide.region_15.16_spmd, body=%wide.region_11.15_spmd.sunk | while | flops 139113216 | bytes 9696951 | solution.py:178
  187.7 1.1 constant_dynamic-slice_fusion.2
  189.4 0.7 fusion.63
  192.2 1.1 constant_dynamic-slice_fusion.2
  193.9 0.7 fusion.63
  196.7 1.1 constant_dynamic-slice_fusion.2
  198.4 0.7 fusion.63
  201.3 1.1 constant_dynamic-slice_fusion.2
  202.9 0.7 fusion.63
  205.8 1.1 constant_dynamic-slice_fusion.2
  207.4 0.7 fusion.63
  210.3 1.1 constant_dynamic-slice_fusion.2
  211.9 0.7 fusion.63
  214.7 1.1 constant_dynamic-slice_fusion.2
  216.4 0.7 fusion.63
  219.2 1.1 constant_dynamic-slice_fusion.2
  220.9 0.7 fusion.63
  223.7 1.1 constant_dynamic-slice_fusion.2
  228.2 1.1 constant_dynamic-slice_fusion.2
  232.7 1.1 constant_dynamic-slice_fusion.2
  237.2 1.1 constant_dynamic-slice_fusion.2
  240.5 1.1 fusion.48
  241.6 51.7 %reduce-scatter.2.cloned.1.call-done = f32[64,512]{1,0:T(8,128)} async-done(((f32[64,2048]{1,0:T(8,128)}), f32[64,512]{1,0:T(8,128)}) %reduce-scatter.2.cloned.1.call-update) | async-done | bytes 131088 | tf_op jit(solution)/shard_map/reduce_scatter | solution.py:185
  293.3 1.5 convert_element_type.84
  (283 shorter events, 39.4 us)
Async XLA Ops:
  6.5 233.9 %copy-start = (bf16[256,2048]{1,0:T(8,128)(2,1)S(1)}, bf16[256,2048]{1,0:T(8,128)(2,1)}, u32[]{:S(2)}) copy-start(bf16[256,2048]{1,0:T(8,128)(2,1)} %param.17) | copy-start | bytes 3145732
  11.7 18.1 %copy-start.5 = (s32[64]{0:T(128)S(1)}, s32[64]{0:T(128)}, u32[]{:S(2)}) copy-start(s32[64]{0:T(128)} %param.21) | copy-start | bytes 772
  11.7 18.6 %copy-start.6 = (s32[64]{0:T(128)S(1)}, s32[64]{0:T(128)}, u32[]{:S(2)}) copy-start(s32[64]{0:T(128)} %param.22) | copy-start | bytes 772
  11.7 18.8 %copy-start.9 = (s32[64]{0:T(128)S(1)}, s32[64]{0:T(128)}, u32[]{:S(2)}) copy-start(s32[64]{0:T(128)} %param.23) | copy-start | bytes 772
  11.7 19.0 %copy-start.3 = (s32[384]{0:T(512)S(1)}, s32[384]{0:T(512)}, u32[]{:S(2)}) copy-start(s32[384]{0:T(512)} %param.20) | copy-start | bytes 4612
  11.7 19.0 %copy-start.4 = (s32[384]{0:T(512)S(1)}, s32[384]{0:T(512)}, u32[]{:S(2)}) copy-start(s32[384]{0:T(512)} %param.19) | copy-start | bytes 4612
  11.7 19.4 %copy-start.1 = (bf16[64,2048]{1,0:T(8,128)(2,1)S(1)}, bf16[64,2048]{1,0:T(8,128)(2,1)}, u32[]{:S(2)}) copy-start(bf16[64,2048]{1,0:T(8,128)(2,1)} %param.13) | copy-start | bytes 786436
  11.7 19.5 %copy-start.7 = (bf16[2048,64]{0,1:T(8,128)(2,1)S(1)}, bf16[2048,64]{0,1:T(8,128)(2,1)}, u32[]{:S(2)}) copy-start(bf16[2048,64]{0,1:T(8,128)(2,1)} %param.15) | copy-start | bytes 786436
  11.7 20.2 %copy-start.8 = (bf16[2048,64]{0,1:T(8,128)(2,1)S(1)}, bf16[2048,64]{0,1:T(8,128)(2,1)}, u32[]{:S(2)}) copy-start(bf16[2048,64]{0,1:T(8,128)(2,1)} %param.16) | copy-start | bytes 786436
  11.7 34.6 %copy-start.2 = (bf16[2048,256]{1,0:T(8,128)(2,1)S(1)}, bf16[2048,256]{1,0:T(8,128)(2,1)}, u32[]{:S(2)}) copy-start(bf16[2048,256]{1,0:T(8,128)(2,1)} %param.14) | copy-start | bytes 3145732
  11.8 174.4 %all-to-all-start = ((bf16[128,1,3,64,128]{4,3,2,1,0:T(8,128)(2,1)}), bf16[128,1,3,64,128]{4,3,2,1,0:T(8,128)(2,1)}, u32[]{:S(2)}, u32[]{:S(2)}) async-start(bf16[128,1,3,64,128]{4,3,2,1,0:T(8,128)(2,1)} %stack.5), calls=%async_computation | async-start | bytes 12582912 | tf_op jit(solution)/shard_map/all_to_all | solution.py:17
  29.7 263.6 %reduce-scatter.2.cloned.1.call-start = ((), (), s32[]{:S(2)}) async-start(), calls=%async_computation.2 | async-start | bytes 655360 | tf_op jit(solution)/shard_map/reduce_scatter | solution.py:185
  32.3 152.1 %collective-permute-start = (bf16[64,1,128]{2,0,1:T(8,128)(2,1)S(1)}, bf16[64,1,128]{2,0,1:T(8,128)(2,1)S(1)}, u32[]{:S(2)}, u32[]{:S(2)}) collective-permute-start(bf16[64,1,128]{2,0,1:T(8,128)(2,1)S(1)} %pad_maximum_fusion.1), channel_id=1, source_target_pairs={{0,4},{1,5},{2,6},{3,7},{4,8},{5,9},{6,10},{7,11},{8,12},{9,13},{1... | collective-permute-start | bytes 49160 | tf_op jit(solution)/shard_map/ppermute | solution.py:23
  36.6 147.8 %collective-permute-start.1 = (bf16[64,1,128]{2,0,1:T(8,128)(2,1)S(1)}, bf16[64,1,128]{2,0,1:T(8,128)(2,1)S(1)}, u32[]{:S(2)}, u32[]{:S(2)}) collective-permute-start(bf16[64,1,128]{2,0,1:T(8,128)(2,1)S(1)} %pad_maximum_fusion.1), channel_id=1, source_target_pairs={{0,3},{1,4},{2,5},{3,6},{4,7},{5,8},{6,9},{7,10},{8,11},{9,12},{10... | collective-permute-start | bytes 49160 | tf_op jit(solution)/shard_map/ppermute | solution.py:23
  39.5 145.0 %collective-permute-start.2 = (bf16[64,1,128]{2,0,1:T(8,128)(2,1)S(1)}, bf16[64,1,128]{2,0,1:T(8,128)(2,1)S(1)}, u32[]{:S(2)}, u32[]{:S(2)}) collective-permute-start(bf16[64,1,128]{2,0,1:T(8,128)(2,1)S(1)} %pad_maximum_fusion.1), channel_id=1, source_target_pairs={{0,2},{1,3},{2,4},{3,5},{4,6},{5,7},{6,8},{7,9},{8,10},{9,11},{10,... | collective-permute-start | bytes 49160 | tf_op jit(solution)/shard_map/ppermute | solution.py:23
  44.1 140.4 %collective-permute-start.3 = (bf16[64,1,128]{2,0,1:T(8,128)(2,1)S(1)}, bf16[64,1,128]{2,0,1:T(8,128)(2,1)S(1)}, u32[]{:S(2)}, u32[]{:S(2)}) collective-permute-start(bf16[64,1,128]{2,0,1:T(8,128)(2,1)S(1)} %pad_maximum_fusion.1), channel_id=1, source_target_pairs={{0,1},{1,2},{2,3},{3,4},{4,5},{5,6},{6,7},{7,8},{8,9},{9,10},{10,1... | collective-permute-start | bytes 49160 | tf_op jit(solution)/shard_map/ppermute | solution.py:23
Sparse Core Ops, SparseCore 0:
  241.7 51.5 reduce-scatter.1
